TPU v7x, 512 devices: a whole 4x4x16 slice. The times are simulated.
512 devices in a mesh: section: 16 (over x, y_hi, core), ctx: 32 (over z, y_lo).
Axes of the slice: x: 4, y: 4 (y_hi: 2, y_lo: 2; y = y_hi * 2 + y_lo), z: 16, core: 2. Of those that a mesh axis runs over, the one named last changes fastest.
Arguments:
- handoff: bfloat16 [16, 2, 3072, 4096], P('section', None, 'ctx'), may hold values from -500 to 500
- norm_gain: bfloat16 [16, 4096], P('section'), may hold values from 0.099609375 to 1.8984375
- kv_weight: bfloat16 [16, 4096, 1024], P('section', 'ctx'), may hold values from -0.09375 to 0.09375
- queries: bfloat16 [16, 2, 3072, 4096], P('section', None, 'ctx'), may hold values from -120 to 120
- span_order: int32 [2, 64], replicated, may hold values from 0 to 63, each once within a row
Outputs:
- partial_out: bfloat16 [16, 2, 3072, 4096], P('section', None, 'ctx')
- log_sum: float32 [16, 2, 32, 3072], P('section', None, None, 'ctx')
Inputs may be any that keep to these rules, and one draw needn't show every extreme that they name: Each row of span_order names every span of 0 to 63 once.
All inputs are finite; a program needn't handle non-finite values.
Results may differ from a plain program's by a relative error of at most 0.012.
The roundings to bfloat16 on the way count: a program that leaves them out, or rounds other values in their place, can miss the bound.
Values may be sent and summed in bfloat16 or wider, within the bound.
A program may use at most 64 MiB of HBM per device.

v0:
```python
import jax
import jax.numpy as jnp
from jax import lax
from jax.sharding import PartitionSpec as P

QH = 32
KVH = 4
HD = 128
WINDOW = 4


rope_base = 500000.0


def passed_along(block, axis, distance):
    devices = range(lax.axis_size(axis))
    route = [((i - distance) % len(devices), i) for i in devices]
    return lax.ppermute(block, axis, route)


def rotate(key_vecs, positions):
    half_dim = key_vecs.shape[-1] // 2
    frequency = rope_base ** (-2.0 * jnp.arange(half_dim, dtype=jnp.float32) / key_vecs.shape[-1])
    angles = positions.astype(jnp.float32)[..., None, None] * frequency
    cosine = jnp.cos(angles)
    sine_part = jnp.sin(angles)
    first_half = key_vecs[..., :half_dim]
    second = key_vecs[..., half_dim:]
    return jnp.concatenate(
        [first_half * cosine - second * sine_part, second * cosine + first_half * sine_part],
        axis=-1,
    )


def on_device(handoff, norm_gain, kv_weight, queries, span_order):
    layer_in = passed_along(handoff, "section", 1)
    micro_count, tok_rows, model_width = (layer_in.shape[1], layer_in.shape[2], layer_in.shape[3])
    activations = layer_in[0].astype(jnp.float32)
    scale = lax.rsqrt(jnp.mean(activations * activations, axis=-1, keepdims=True) + 1e-05)
    normed = (activations * scale * norm_gain[0].astype(jnp.float32)).astype(jnp.bfloat16)
    flat_rows = normed.reshape(micro_count * tok_rows, model_width)
    weight = kv_weight[0]
    kv_width = weight.shape[1] // 2

    def add_rows(shard_rows):
        return jnp.dot(flat_rows, shard_rows, preferred_element_type=jnp.float32)

    key_part = add_rows(lax.all_gather(weight[:, :kv_width], "ctx", axis=0, tiled=True))
    value_part = add_rows(lax.all_gather(weight[:, kv_width:], "ctx", axis=0, tiled=True))
    cycle_size = lax.axis_size("ctx")
    own_index = lax.axis_index("ctx")
    span_len = tok_rows // 2

    def device_positions(device):
        span_ids = lax.dynamic_slice_in_dim(span_order, 2 * device, 2, 1)
        spread = (
            span_ids[:, :, None] * span_len + jnp.arange(span_len, dtype=jnp.int32)[None, None, :]
        )
        return spread.reshape(micro_count, tok_rows)

    own_pos = device_positions(own_index)
    key_vecs = rotate(key_part.reshape(micro_count, tok_rows, KVH, HD), own_pos)
    kv_block = jnp.concatenate(
        [
            key_vecs.reshape(micro_count, tok_rows, kv_width),
            value_part.reshape(micro_count, tok_rows, kv_width),
        ],
        axis=-1,
    ).astype(jnp.bfloat16)
    blocks = [kv_block]
    current = kv_block
    for step_num in range(1, WINDOW):
        current = passed_along(current, "ctx", 1)
        blocks.append(current)
    window_kv = jnp.concatenate(blocks, axis=1)
    window_pos = jnp.concatenate(
        [device_positions((own_index - step_num) % cycle_size) for step_num in range(WINDOW)],
        axis=1,
    )
    group_size = QH // KVH
    query_block = queries[0].reshape(micro_count, tok_rows, KVH, group_size, HD)
    results = []
    log_sums = []
    for micro_idx in range(micro_count):
        key_rows = window_kv[micro_idx, :, :kv_width].reshape(-1, KVH, HD)
        value_rows = window_kv[micro_idx, :, kv_width:].reshape(-1, KVH, HD)
        scores = jnp.einsum(
            "tkgd,ukd->kgtu", query_block[micro_idx], key_rows, preferred_element_type=jnp.float32
        ) * HD ** (-0.5)
        visible = (
            window_pos[micro_idx][None, None, None, :] <= own_pos[micro_idx][None, None, :, None]
        )
        scores = jnp.where(visible, scores, -jnp.inf)
        row_max = jnp.max(scores, axis=-1, keepdims=True)
        exps = jnp.exp(scores - row_max)
        running = jnp.sum(exps, axis=-1, keepdims=True)
        weights_bf = exps.astype(jnp.bfloat16)
        mixed = jnp.einsum(
            "kgtu,ukd->tkgd", weights_bf, value_rows, preferred_element_type=jnp.float32
        )
        denominator = jnp.moveaxis(running[..., 0], 2, 0)[..., None]
        results.append((mixed / denominator).astype(jnp.bfloat16).reshape(tok_rows, QH * HD))
        log_sums.append((row_max + jnp.log(running))[..., 0].reshape(QH, tok_rows))
    return (jnp.stack(results)[None], jnp.stack(log_sums)[None])


def solution(mesh):
    placed = (
        P("section", None, "ctx", None),
        P("section", None),
        P("section", "ctx", None),
        P("section", None, "ctx", None),
        P(),
    )
    return jax.shard_map(
        on_device,
        mesh=mesh,
        in_specs=placed,
        out_specs=(P("section", None, "ctx", None), P("section", None, None, "ctx")),
        check_vma=False,
    )
```

profile of v0, /device:TPU:6, one launch (start us, length us, event | category | flops | bytes accessed | tf_op | source)
XLA Modules:
  0.0 375.5 jit_solution(1482915106801693712)
XLA Ops:
  7.2 1.7 fusion.64
  9.0 0.7 all-gather.5.cloned.1.call-update
  9.7 1.9 collective-permute-start
  11.7 0.9 fusion.55
  13.0 0.1 add.201
  13.2 0.1 add.206
  13.3 0.1 add.211
  13.5 0.7 convert_element_type.75
  14.3 0.4 multiply_cosine_fusion
  14.7 19.3 %collective-permute-done = bf16[1,2,96,4096]{3,2,1,0:T(8,128)(2,1)S(1)} collective-permute-done((bf16[1,2,96,4096]{3,2,1,0:T(8,128)(2,1)}, bf16[1,2,96,4096]{3,2,1,0:T(8,128)(2,1)S(1)}, u32[]{:S(2)}, u32[]{:S(2)}) %collective-permute-start) | collective-permute-done | bytes 1572896 | tf_op jit(solution)/shard_map/ppermute | solution.py:18
  34.0 0.4 fusion.10
  34.4 122.0 %all-gather.3.cloned.1.call-done = bf16[4096,512]{1,0:T(8,128)(2,1)} async-done(((bf16[128,512]{1,0:T(8,128)(2,1)}), bf16[4096,512]{1,0:T(8,128)(2,1)}) %all-gather.3.cloned.1.call-update) | async-done | bytes 4194320 | tf_op jit(solution)/shard_map/all_gather | solution.py:48
  156.4 6.4 %copy.12 = bf16[512,4096]{1,0:T(8,128)(2,1)} copy(bf16[512,4096]{0,1:T(8,128)(2,1)} %bitcast.98) | data formatting | bytes 8388608 | tf_op jit(solution)/shard_map/dot_general | solution.py:46
  162.8 3.7 fusion.28
  166.6 0.2 subtract_convert_fusion
  166.8 0.1 copy_bitcast_fusion
  166.9 136.3 %all-gather.5.cloned.1.call-done = bf16[4096,512]{1,0:T(8,128)(2,1)} async-done(((bf16[128,512]{1,0:T(8,128)(2,1)}), bf16[4096,512]{1,0:T(8,128)(2,1)}) %all-gather.5.cloned.1.call-update) | async-done | bytes 4194320 | tf_op jit(solution)/shard_map/all_gather | solution.py:49
  303.2 3.2 fusion.41
  306.5 1.9 collective-permute-start.1
  308.5 13.1 %collective-permute-done.1 = bf16[2,96,1024]{2,1,0:T(8,128)(2,1)S(1)} collective-permute-done((bf16[2,96,1024]{2,1,0:T(8,128)(2,1)S(1)}, bf16[2,96,1024]{2,1,0:T(8,128)(2,1)S(1)}, u32[]{:S(2)}, u32[]{:S(2)}) %collective-permute-start.1) | collective-permute-done | bytes 393248 | tf_op jit(solution)/shard_map/ppermute | solution.py:18
  321.6 1.9 collective-permute-start.2
  323.5 0.1 slice_bitcast_fusion.1
  323.7 9.8 %collective-permute-done.2 = bf16[2,96,1024]{2,1,0:T(8,128)(2,1)} collective-permute-done((bf16[2,96,1024]{2,1,0:T(8,128)(2,1)S(1)}, bf16[2,96,1024]{2,1,0:T(8,128)(2,1)}, u32[]{:S(2)}, u32[]{:S(2)}) %collective-permute-start.2) | collective-permute-done | bytes 393248 | tf_op jit(solution)/shard_map/ppermute | solution.py:18
  333.4 2.2 collective-permute-start.3
  335.9 0.2 copy.36
  336.1 0.2 copy.37
  336.3 0.7 broadcast_compare_fusion
  337.0 8.6 %collective-permute-done.3 = bf16[2,96,1024]{2,1,0:T(8,128)(2,1)} collective-permute-done((bf16[2,96,1024]{2,1,0:T(8,128)(2,1)}, bf16[2,96,1024]{2,1,0:T(8,128)(2,1)}, u32[]{:S(2)}, u32[]{:S(2)}) %collective-permute-start.3) | collective-permute-done | bytes 393248 | tf_op jit(solution)/shard_map/ppermute | solution.py:18
  345.7 1.2 pad_maximum_fusion
  346.9 0.1 fusion.63
  347.0 0.1 reshape_squeeze.14
  347.2 2.0 fusion.8
  349.2 2.1 copy-done.1
  351.3 1.5 fusion.2
  352.9 0.1 reshape_squeeze.16
  353.0 1.2 fusion.9
  354.2 2.2 copy-done
  356.3 1.5 fusion.4
  357.9 0.1 reshape_squeeze.13
  358.0 3.7 fusion.32
  361.7 0.3 copy.17
  362.0 0.3 stack_reshape.6
  362.3 0.1 reshape_squeeze.15
  362.4 3.7 fusion.31
  366.1 0.3 copy.21
  366.4 0.3 stack_reshape.7
  366.8 0.6 maximum_bitcast_fusion.2
  367.4 1.3 maximum_bitcast_fusion
  (42 shorter events, 1.2 us)
Async XLA Ops:
  7.2 149.3 %all-gather.3.cloned.1.call-start = ((), (), s32[]{:S(2)}) async-start(), calls=%async_computation | async-start | bytes 4325376 | tf_op jit(solution)/shard_map/all_gather | solution.py:48
  8.9 294.3 %all-gather.5.cloned.1.call-start = ((), (), s32[]{:S(2)}) async-start(), calls=%async_computation.1 | async-start | bytes 4325376 | tf_op jit(solution)/shard_map/all_gather | solution.py:49
  9.7 24.4 %collective-permute-start = (bf16[1,2,96,4096]{3,2,1,0:T(8,128)(2,1)}, bf16[1,2,96,4096]{3,2,1,0:T(8,128)(2,1)S(1)}, u32[]{:S(2)}, u32[]{:S(2)}) collective-permute-start(bf16[1,2,96,4096]{3,2,1,0:T(8,128)(2,1)} %param.5), channel_id=1, source_target_pairs={{480,0},{0,32},{32,64},{64,96},{96,128},{128,160},{160,192},{192,2... | collective-permute-start | bytes 4718600 | tf_op jit(solution)/shard_map/ppermute | solution.py:18
  166.9 156.6 %copy-start.2 = (bf16[1,2,96,4096]{3,2,1,0:T(8,128)(2,1)S(1)}, bf16[1,2,96,4096]{3,2,1,0:T(8,128)(2,1)}, u32[]{:S(2)}) copy-start(bf16[1,2,96,4096]{3,2,1,0:T(8,128)(2,1)} %param.8) | copy-start | bytes 4718596
  306.4 17.3 %copy-start.3 = (bf16[2,96,512]{2,1,0:T(8,128)(2,1)}, bf16[2,96,512]{2,1,0:T(8,128)(2,1)S(1)}, u32[]{:S(2)}) copy-start(bf16[2,96,512]{2,1,0:T(8,128)(2,1)S(1)} %fusion.41) | copy-start | bytes 589828
  306.5 15.1 %collective-permute-start.1 = (bf16[2,96,1024]{2,1,0:T(8,128)(2,1)S(1)}, bf16[2,96,1024]{2,1,0:T(8,128)(2,1)S(1)}, u32[]{:S(2)}, u32[]{:S(2)}) collective-permute-start(bf16[2,96,1024]{2,1,0:T(8,128)(2,1)S(1)} %pad_maximum_fusion.1), channel_id=1, source_target_pairs={{31,0},{0,1},{1,2},{2,3},{3,4},{4,5},{5,6},{6,7},{7,8},{8,9},{9,10... | collective-permute-start | bytes 1179656 | tf_op jit(solution)/shard_map/ppermute | solution.py:18
  321.6 11.9 %copy-start.5 = (bf16[2,96,1024]{2,1,0:T(8,128)(2,1)}, bf16[2,96,1024]{2,1,0:T(8,128)(2,1)S(1)}, u32[]{:S(2)}) copy-start(bf16[2,96,1024]{2,1,0:T(8,128)(2,1)S(1)} %collective-permute-done.1) | copy-start | bytes 1179652
  321.6 11.9 %collective-permute-start.2 = (bf16[2,96,1024]{2,1,0:T(8,128)(2,1)S(1)}, bf16[2,96,1024]{2,1,0:T(8,128)(2,1)}, u32[]{:S(2)}, u32[]{:S(2)}) collective-permute-start(bf16[2,96,1024]{2,1,0:T(8,128)(2,1)S(1)} %collective-permute-done.1), channel_id=1, source_target_pairs={{31,0},{0,1},{1,2},{2,3},{3,4},{4,5},{5,6},{6,7},{7,8},{8,9},{9,10... | collective-permute-start | bytes 1179656 | tf_op jit(solution)/shard_map/ppermute | solution.py:18
  333.4 12.2 %copy-start.4 = (bf16[2,96,512]{2,1,0:T(8,128)(2,1)S(1)}, bf16[2,96,512]{2,1,0:T(8,128)(2,1)}, u32[]{:S(2)}) copy-start(bf16[2,96,512]{2,1,0:T(8,128)(2,1)} %copy-done.3) | copy-start | bytes 589828
  333.4 12.2 %collective-permute-start.3 = (bf16[2,96,1024]{2,1,0:T(8,128)(2,1)}, bf16[2,96,1024]{2,1,0:T(8,128)(2,1)}, u32[]{:S(2)}, u32[]{:S(2)}) collective-permute-start(bf16[2,96,1024]{2,1,0:T(8,128)(2,1)} %collective-permute-done.2), channel_id=1, source_target_pairs={{31,0},{0,1},{1,2},{2,3},{3,4},{4,5},{5,6},{6,7},{7,8},{8,9},{9,10... | collective-permute-start | bytes 1179656 | tf_op jit(solution)/shard_map/ppermute | solution.py:18
  335.9 9.8 %copy-start.6 = (bf16[2,96,1024]{2,1,0:T(8,128)(2,1)S(1)}, bf16[2,96,1024]{2,1,0:T(8,128)(2,1)}, u32[]{:S(2)}) copy-start(bf16[2,96,1024]{2,1,0:T(8,128)(2,1)} %copy-done.5) | copy-start | bytes 1179652
  347.1 4.2 %copy-start.8 = (pred[96,384]{1,0:T(8,128)(4,1)S(1)}, pred[96,384]{1,0:T(8,128)(4,1)}, u32[]{:S(2)}) copy-start(pred[96,384]{1,0:T(8,128)(4,1)} %get-tuple-element.33) | copy-start | bytes 110596
  349.2 2.1 copy-start.1
  349.2 3.8 %copy-start.7 = (pred[96,384]{1,0:T(8,128)(4,1)S(1)}, pred[96,384]{1,0:T(8,128)(4,1)}, u32[]{:S(2)}) copy-start(pred[96,384]{1,0:T(8,128)(4,1)} %get-tuple-element.32) | copy-start | bytes 110596
  354.2 2.2 copy-start
  354.2 3.8 %copy-start.9 = (pred[96,384]{1,0:T(8,128)(4,1)S(1)}, pred[96,384]{1,0:T(8,128)(4,1)}, u32[]{:S(2)}) copy-start(pred[96,384]{1,0:T(8,128)(4,1)} %get-tuple-element.33) | copy-start | bytes 110596
Sparse Core Ops, SparseCore 0:
  10.7 145.7 all-gather.2
  158.5 144.6 all-gather.4
where the time goes:
time: 378 us; the launch traced here: 376 us
  waiting for transfers between devices  310 us (82%)
  matrix products  17.5 us (5%)
  local copies, waits for them, and re-layouts  15.6 us (4%)
  between operations  14.5 us (4%)
  other arithmetic  10 us (3%)
  starting transfers between devices  8.06 us (2%)
    all_gather x1, waiting for transfers between devices, on_device(): lax.all_gather(weight[:, kv_width:], 'ctx', axis=0, tiled=True)  136 us
    all_gather x1, waiting for transfers between devices, on_device(): lax.all_gather(weight[:, :kv_width], 'ctx', axis=0, tiled=True)  122 us
    ppermute x4, waiting for transfers between devices, passed_along(): return lax.ppermute(block, axis, route)  50.9 us
    ppermute x4, starting transfers between devices, passed_along(): return lax.ppermute(block, axis, route)  7.98 us
  transfers between devices with their start and end apart: 6, of which 6 were waited for; matrix products, arithmetic and copies ran while one was open for 4% of the time, Pallas kernels for 0%

commit v1 on v0

v1 whole, which is shorter than its diff:
```python
import functools
import math

import jax
import jax.numpy as jnp
import numpy as np
from jax import lax
from jax.experimental import pallas as pl
from jax.experimental.pallas import tpu as pltpu
from jax.sharding import PartitionSpec as P

QH = 32
KVH = 4
HD = 128
GROUP = QH // KVH
SPAN = 48
TOK = 96
MB = 2
D = 4096
ROWS = MB * TOK
WIN = 5 * TOK
SEEN = 4 * TOK
MESH = pl.DeviceIdType.MESH
PARTS = 4
PART = ROWS // PARTS
LAG = 8
LOG2E = math.log2(math.e)
LN2 = math.log(2.0)
rope_base = 500000.0


def kernel(
    sections, ring,
    order, freq, gain, hand, weight, queries,
    out, lse,
    x_buf, xn, w_buf, acc, win, q_buf, o_buf, probs, recip, cosine, sine, bias, lbuf,
    loc_sem, w_recv, w_up, w_dn, w_mate, x_recv, x_send, win_recv, win_send, out_sem,
):
    s = lax.axis_index("section")
    c = lax.axis_index("ctx")
    z = c // 2
    y = lax.rem(c, 2)
    other = 1 - y
    mate = 2 * z + other
    half = ring // 2
    even = lax.rem(s, 2) == 0
    nxt = lax.rem(s + 1, sections)
    prv = lax.rem(s + sections - 1, sections)

    def at_z(step):
        return lax.rem(z + step + ring, ring)

    up = {"ctx": 2 * at_z(1) + y}
    dn = {"ctx": 2 * at_z(-1) + y}
    far = {"ctx": 2 * at_z(2)}
    back = at_z(-2)
    mate_id = {"ctx": mate}

    barrier = pltpu.get_barrier_semaphore()

    def greet(device):
        pl.semaphore_signal(barrier, inc=1, device_id=device, device_id_type=MESH)

    for device in (
        up, dn, mate_id,
        {"section": nxt, "ctx": c}, {"section": prv, "ctx": c},
        {"section": nxt, "ctx": mate}, {"section": prv, "ctx": mate},
        far,
    ):
        greet(device)

    @pl.when(y == 0)
    def _():
        greet({"ctx": 2 * back})
        greet({"ctx": 2 * back + 1})
        pl.semaphore_wait(barrier, 10)

    @pl.when(y == 1)
    def _():
        pl.semaphore_wait(barrier, 8)

    def remote(src, dst, send, recv, device):
        return pltpu.make_async_remote_copy(
            src_ref=src, dst_ref=dst, send_sem=send, recv_sem=recv,
            device_id=device, device_id_type=MESH,
        )

    def w_cols(p, h):
        return weight.at[:, pl.ds(pl.multiple_of(p * 512 + h * 256, 256), 256)]

    def w_slot(p, chunk, b):
        return w_buf.at[p, chunk, pl.ds(pl.multiple_of(b * 128, 128), 128)]

    def w_local(p):
        return pltpu.make_async_copy(w_cols(p, y), w_slot(p, z, y), loc_sem.at[p])

    def w_cross(p, b):
        return remote(w_cols(p, other), w_slot(p, z, b), w_mate.at[p], w_recv.at[p, z, b], mate_id)

    for p in range(2):
        w_local(p).start()
        w_cross(p, y).start()

    def x_rows(b, r):
        return x_buf.at[b, pl.ds(r * PART, PART)]

    def x_copy(kind, src, b, r, device):
        return remote(src, x_rows(b, r), x_send.at[kind, r], x_recv.at[b, r], device)

    def x_cross(r):
        return x_copy(0, hand.at[pl.ds(r * PART, PART)], y, r, {"section": nxt, "ctx": mate})

    def x_direct(r):
        return x_copy(1, hand.at[pl.ds(r * PART, PART)], y, r, {"section": nxt, "ctx": c})

    def x_onward(r):
        return x_copy(2, x_rows(other, r), other, r, mate_id)

    def x_arrived(b, r):
        x_copy(0, x_rows(b, r), b, r, mate_id).wait_recv()

    for r in range(PARTS):
        x_cross(r).start()

        @pl.when(even)
        def _():
            x_direct(r).start()

    q_copy = pltpu.make_async_copy(queries, q_buf, loc_sem.at[2])
    q_copy.start()

    def w_hop(p, k, b, upward):
        chunk = at_z(-k if upward else k)
        sems = w_up if upward else w_dn
        slot = w_slot(p, chunk, b)
        return remote(slot, slot, sems.at[p, k, b], w_recv.at[p, chunk, b], up if upward else dn)

    def ring_step(p, k):
        for b in (y, other):
            if k == 0:
                if b is y:
                    w_local(p).wait()
                else:
                    w_cross(p, other).wait_recv()
            else:
                if k < half:
                    w_hop(p, k, b, True).wait_recv()
                w_hop(p, k, b, False).wait_recv()
            if k < half - 1:
                w_hop(p, k, b, True).start()
            if k < half:
                w_hop(p, k, b, False).start()

    def slots(p, h, first, count):
        return win.at[p, pl.ds(2 * h, 2), :, pl.ds(first * TOK, count * TOK)]

    def to_up(p):
        return remote(slots(p, y, 3, 2), slots(p, y, 1, 2), win_send.at[p, 0], win_recv.at[p, 0], up)

    def to_far(p, h):
        return remote(slots(p, y, 4, 1), slots(p, h, 0, 1), win_send.at[p, 1], win_recv.at[p, 1 + h], far)

    def to_mate(p, h):
        return remote(slots(p, h, 3, 1), slots(p, h, 3, 1), win_send.at[p, 2], win_recv.at[p, 3], mate_id)

    def to_mate_last(p, h):
        return remote(slots(p, h, 4, 1), slots(p, h, 4, 1), win_send.at[p, 3], win_recv.at[p, 4], mate_id)

    def to_mate_old(p, h):
        return remote(slots(p, h, 1, 2), slots(p, h, 1, 2), win_send.at[p, 4], win_recv.at[p, 5], mate_id)

    def window_out(p):
        to_up(p).start()
        to_mate(p, y).start()

        @pl.when(y == 0)
        def _():
            to_mate_last(p, y).start()

        to_far(p, y).start()

    def window_onward(p):
        to_up(p).wait_recv()
        to_mate_old(p, y).start()

    def window_arrived(p):
        to_mate(p, other).wait_recv()
        to_mate_old(p, other).wait_recv()

        @pl.when(y == 0)
        def _():
            to_far(p, 0).wait_recv()
            to_far(p, 1).wait_recv()

        @pl.when(y == 1)
        def _():
            to_mate_last(p, other).wait_recv()

    def tables():
        row = lax.broadcasted_iota(jnp.int32, (SPAN, HD), 0)
        low = lax.broadcasted_iota(jnp.int32, (SPAN, HD), 1) < HD // 2
        for b in range(2):
            for m in range(MB):
                for i in range(2):
                    span = order[m, 4 * z + 2 * b + i]
                    angle = (span * SPAN + row).astype(jnp.float32) * freq[...]
                    first = b * ROWS + m * TOK + i * SPAN
                    cosine[pl.ds(first, SPAN), :] = jnp.cos(angle)
                    turned = jnp.sin(angle)
                    sine[pl.ds(first, SPAN), :] = jnp.where(low, -turned, turned)

    def masks():
        lane = lax.broadcasted_iota(jnp.int32, (SPAN, SEEN), 1)
        row = lax.broadcasted_iota(jnp.int32, (SPAN, SEEN), 0)
        for m in range(MB):
            key_pos = lane
            for j in range(4):
                block = lax.rem(c - 3 + j + 2 * ring, 2 * ring)
                for i in range(2):
                    n = 2 * j + i
                    here = lane >= n * SPAN
                    key_pos = jnp.where(here, order[m, 2 * block + i] * SPAN + lane - n * SPAN, key_pos)
            for i in range(2):
                own_pos = order[m, 2 * c + i] * SPAN + row
                bias[m, pl.ds(i * SPAN, SPAN), :] = jnp.where(key_pos <= own_pos, 0.0, -jnp.inf)

    def normalise(b, r):
        first = pl.multiple_of(b * ROWS + r * PART, 16)
        values = x_buf[b, pl.ds(r * PART, PART), :].astype(jnp.float32)
        scale = lax.rsqrt(jnp.mean(values * values, axis=-1, keepdims=True) + 1e-05)
        scaled = values * scale * gain[...].astype(jnp.float32)
        xn[pl.ds(first, PART), :] = scaled.astype(jnp.bfloat16)

    def product(p, chunk):
        columns = pl.ds(pl.multiple_of(chunk * 256, 256), 256)
        return jnp.dot(xn[:, columns], w_buf[p, chunk], preferred_element_type=jnp.float32)

    def keys():
        acc[...] = jnp.zeros_like(acc)

        def add(chunk, _):
            acc[...] += product(0, chunk)
            return 0

        lax.fori_loop(0, ring, add, 0)
        for sub in range(2):
            part = acc[:, sub * HD : (sub + 1) * HD]
            turned = part * cosine[...] + pltpu.roll(part, HD // 2, 1) * sine[...]
            store(0, sub, turned)
        acc[...] = jnp.zeros_like(acc)

    def store(p, sub, rows):
        rows = rows.astype(jnp.bfloat16)
        for b in range(2):
            for m in range(MB):
                win[p, 2 * y + sub, m, pl.ds((3 + b) * TOK, TOK), :] = rows[
                    b * ROWS + m * TOK : b * ROWS + (m + 1) * TOK
                ]

    def value_step(k):
        if k < half:
            acc[...] += product(1, at_z(-k))
        if k > 0:
            acc[...] += product(1, at_z(k))

    def score(n, _):
        m = lax.rem(n, MB)
        head = lax.rem(2 * y + n // MB, KVH)
        q = jnp.concatenate(
            [
                q_buf[pl.ds(pl.multiple_of(m * TOK, TOK), TOK), pl.ds(pl.multiple_of((head * GROUP + g) * HD, HD), HD)]
                for g in range(GROUP)
            ],
            axis=0,
        )
        k = win[0, head, m, pl.ds(pl.multiple_of(y * TOK, TOK), SEEN), :]
        raw = lax.dot_general(q, k, (((1,), (1,)), ((), ())), preferred_element_type=jnp.float32)
        raw = raw.reshape(GROUP, TOK, SEEN) * (HD ** -0.5 * LOG2E) + bias[m][None]
        top = jnp.max(raw, axis=-1, keepdims=True)
        exps = jnp.exp2(raw - top)
        total = jnp.sum(exps, axis=-1, keepdims=True)
        probs[n] = exps.astype(jnp.bfloat16).reshape(GROUP * TOK, SEEN)
        recip[n] = jnp.broadcast_to(1.0 / total, (GROUP, TOK, HD))
        logs = top * LN2 + jnp.log(total)
        lane = lax.broadcasted_iota(jnp.int32, (TOK, HD), 1)
        kept = lbuf[m]
        for g in range(GROUP):
            kept = jnp.where(lane == head * GROUP + g, logs[g], kept)
        lbuf[m] = kept
        return 0

    def out_copy(n):
        m = lax.rem(n, MB)
        head = lax.rem(2 * y + n // MB, KVH)
        view = (
            pl.ds(pl.multiple_of(m * TOK, TOK), TOK),
            pl.ds(pl.multiple_of(head * GROUP * HD, GROUP * HD), GROUP * HD),
        )
        return pltpu.make_async_copy(o_buf.at[view], out.at[view], out_sem.at[n])

    def mix(n, _):
        m = lax.rem(n, MB)
        head = lax.rem(2 * y + n // MB, KVH)
        v = win[1, head, m, pl.ds(pl.multiple_of(y * TOK, TOK), SEEN), :]
        mixed = jnp.dot(probs[n], v, preferred_element_type=jnp.float32)
        mixed = (mixed.reshape(GROUP, TOK, HD) * recip[n]).astype(jnp.bfloat16)
        for g in range(GROUP):
            o_buf[
                pl.ds(pl.multiple_of(m * TOK, TOK), TOK),
                pl.ds(pl.multiple_of((head * GROUP + g) * HD, HD), HD),
            ] = mixed[g]
        out_copy(n).start()
        return 0

    def onward(r):
        @pl.when(even)
        def _():
            x_arrived(other, r)
            x_onward(r).start()

    def ready(b, r):
        if b is other:
            @pl.when(jnp.logical_not(even))
            def _():
                x_arrived(other, r)
        else:
            x_arrived(y, r)

    for t in range(LAG + half + 1):
        if t <= half:
            ring_step(0, t)
        if 0 <= t - LAG <= half:
            ring_step(1, t - LAG)
        if t == 0:
            tables()
        if t == 1:
            masks()
            lbuf[...] = jnp.zeros_like(lbuf)
        if t in (3, 5, 7, 8):
            onward((3, 5, 7, 8).index(t))
        if t in (9, 10):
            for r in (2 * (t - 9), 2 * (t - 9) + 1):
                ready(other, r)
                normalise(other, r)
        if t in (11, 12):
            for r in (2 * (t - 11), 2 * (t - 11) + 1):
                ready(y, r)
                normalise(y, r)
        if t == 12:
            keys()
            window_out(0)
            for k in range(t - LAG + 1):
                value_step(k)
        if t > 12:
            value_step(t - LAG)
        if t == 15:
            window_onward(0)

    for sub in range(2):
        store(1, sub, acc[:, sub * HD : (sub + 1) * HD])
    window_out(1)
    q_copy.wait()
    window_arrived(0)
    lax.fori_loop(0, KVH, score, 0)
    window_onward(1)
    lax.fori_loop(KVH, MB * KVH, score, 0)
    for m in range(MB):
        lse[m] = lbuf[m].T[:QH, :]
    window_arrived(1)
    lax.fori_loop(0, MB * KVH, mix, 0)

    for p in range(2):
        w_cross(p, y).wait_send()
        for k in range(half):
            for b in range(2):
                if k < half - 1:
                    w_hop(p, k, b, True).wait_send()
                w_hop(p, k, b, False).wait_send()
        to_up(p).wait_send()
        to_far(p, y).wait_send()
        to_mate(p, y).wait_send()
        to_mate_old(p, y).wait_send()

        @pl.when(y == 0)
        def _():
            to_mate_last(p, y).wait_send()

    for r in range(PARTS):
        x_cross(r).wait_send()

        @pl.when(even)
        def _():
            x_direct(r).wait_send()
            x_onward(r).wait_send()

    for n in range(MB * KVH):
        out_copy(n).wait()


def solution(mesh):
    sections, n_ctx = mesh.shape["section"], mesh.shape["ctx"]
    ring = n_ctx // 2
    half = ring // 2

    def on_device(handoff, norm_gain, kv_weight, queries, span_order):
        freq = rope_base ** (-2.0 * np.arange(HD // 2, dtype=np.float64) / HD)
        freq = jnp.asarray(np.concatenate([freq, freq])[None].astype(np.float32))
        any_space = pl.BlockSpec(memory_space=pl.ANY)
        vmem = pl.BlockSpec(memory_space=pltpu.VMEM)
        dma = pltpu.SemaphoreType.DMA
        bf16, f32 = jnp.bfloat16, jnp.float32
        out, lse = pl.pallas_call(
            functools.partial(kernel, sections, ring),
            out_shape=(
                jax.ShapeDtypeStruct((ROWS, D), bf16),
                jax.ShapeDtypeStruct((MB, QH, TOK), f32),
            ),
            in_specs=[pl.BlockSpec(memory_space=pltpu.SMEM), vmem, vmem, any_space, any_space, any_space],
            out_specs=(any_space, vmem),
            scratch_shapes=[
                pltpu.VMEM((2, ROWS, D), bf16),
                pltpu.VMEM((2 * ROWS, D), bf16),
                pltpu.VMEM((2, ring, 256, 256), bf16),
                pltpu.VMEM((2 * ROWS, 256), f32),
                pltpu.VMEM((2, KVH, MB, WIN, HD), bf16),
                pltpu.VMEM((ROWS, D), bf16),
                pltpu.VMEM((ROWS, D), bf16),
                pltpu.VMEM((MB * KVH, GROUP * TOK, SEEN), bf16),
                pltpu.VMEM((MB * KVH, GROUP, TOK, HD), f32),
                pltpu.VMEM((2 * ROWS, HD), f32),
                pltpu.VMEM((2 * ROWS, HD), f32),
                pltpu.VMEM((MB, TOK, SEEN), f32),
                pltpu.VMEM((MB, TOK, HD), f32),
                dma((3,)),
                dma((2, ring, 2)),
                dma((2, half, 2)),
                dma((2, half, 2)),
                dma((2,)),
                dma((2, PARTS)),
                dma((3, PARTS)),
                dma((2, 6)),
                dma((2, 5)),
                dma((MB * KVH,)),
            ],
            compiler_params=pltpu.CompilerParams(
                collective_id=0, has_side_effects=True, vmem_limit_bytes=56 << 20
            ),
            name="relay",
        )(
            span_order, freq, norm_gain, handoff.reshape(ROWS, D), kv_weight[0], queries.reshape(ROWS, D),
        )
        return out.reshape(1, MB, TOK, D), lse[None]

    placed = (
        P("section", None, "ctx", None),
        P("section", None),
        P("section", "ctx", None),
        P("section", None, "ctx", None),
        P(),
    )
    return jax.shard_map(
        on_device,
        mesh=mesh,
        in_specs=placed,
        out_specs=(P("section", None, "ctx", None), P("section", None, None, "ctx")),
        check_vma=False,
    )
```

time: 378 us -> 113 us (0.30)
  the two profiles are of different devices: /device:TPU:6 before, /device:TPU:32 now
where the time goes in v1:
time: 113 us
  Pallas kernels  109 us (96%)
  local copies, waits for them, and re-layouts  3.33 us (3%)
    pallas_call x1, Pallas kernels, on_device(): pl.pallas_call(functools.partial(kernel, sections, ring), out_shape=(jax....  109 us
    unnamed x4, local copies, waits for them, and re-layouts  3.33 us

profile of v1, /device:TPU:32, one launch (start us, length us, event | category | flops | bytes accessed | tf_op | source)
XLA Modules:
  0.0 113.1 jit_solution(713264444067158693)
XLA Ops:
  0.6 109.1 %relay.1 = (bf16[192,4096]{1,0:T(8,128)(2,1)}, f32[2,32,96]{2,1,0:T(8,128)}) custom-call(s32[2,64]{1,0:T(2,128)} %order.1, f32[1,128]{1,0:T(1,128)} %constant.2.clone.freq, bf16[1,4096]{1,0:T(2,128)(2,1)} %gain.1, bf16[192,4096]{1,0:T(8,128)(2,1)} %bitcast.5, bf16[128,1024]{1,0:T(8,128)(2,1)} %bitcast.8, bf16[192,4096]{1,0:T(8,128)(2,1)} %bitcast.6), custom_call_target="tpu_custom_call" | custom-call | tf_op jit(solution)/shard_map/relay/pallas_call | solution.py:412
  109.8 0.0 copy-start
  109.8 2.7 %copy.10 = bf16[1,2,96,4096]{3,2,1,0:T(8,128)(2,1)} copy(bf16[1,2,96,4096]{3,2,1,0:T(8,128)(2,1)} %bitcast.7) | data formatting | bytes 3145728
  112.5 0.0 copy-done
  112.5 0.6 copy.11
Async XLA Ops:
  109.8 2.7 %copy-start = (f32[2,32,96]{2,1,0:T(8,128)S(1)}, f32[2,32,96]{2,1,0:T(8,128)}, u32[]{:S(2)}) copy-start(f32[2,32,96]{2,1,0:T(8,128)} %get-tuple-element.5) | copy-start | bytes 73732

commit v2 on v1

--- a/solution.py
+++ b/solution.py
@@ -23,7 +23,10 @@
 MESH = pl.DeviceIdType.MESH
 PARTS = 4
 PART = ROWS // PARTS
-LAG = 8
+LAG = 1
+SUBS = 2
+ONWARD = (1, 2, 3, 4)
+NORMED = 7
 LOG2E = math.log2(math.e)
 LN2 = math.log(2.0)
 rope_base = 500000.0
@@ -31,10 +34,10 @@
 
 def kernel(
     sections, ring,
-    order, freq, gain, hand, weight, queries,
+    order_in, freq_in, gain_in, hand, weight, queries,
     out, lse,
-    x_buf, xn, w_buf, acc, win, q_buf, o_buf, probs, recip, cosine, sine, bias, lbuf,
-    loc_sem, w_recv, w_up, w_dn, w_mate, x_recv, x_send, win_recv, win_send, out_sem,
+    order, freq, gain, x_buf, xn, w_buf, acc, win, q_buf, probs, recip, cosine, sine, bias, lbuf,
+    loc_sem, w_recv, w_up, w_dn, w_mate, x_recv, x_send, win_recv, win_send,
 ):
     s = lax.axis_index("section")
     c = lax.axis_index("ctx")
@@ -73,11 +76,6 @@
     def _():
         greet({"ctx": 2 * back})
         greet({"ctx": 2 * back + 1})
-        pl.semaphore_wait(barrier, 10)
-
-    @pl.when(y == 1)
-    def _():
-        pl.semaphore_wait(barrier, 8)
 
     def remote(src, dst, send, recv, device):
         return pltpu.make_async_remote_copy(
@@ -95,10 +93,28 @@
         return pltpu.make_async_copy(w_cols(p, y), w_slot(p, z, y), loc_sem.at[p])
 
     def w_cross(p, b):
-        return remote(w_cols(p, other), w_slot(p, z, b), w_mate.at[p], w_recv.at[p, z, b], mate_id)
-
+        return remote(w_cols(p, other), w_slot(p, z, b), w_mate.at[p], w_recv.at[p, z, b, 0], mate_id)
+
+    fetches = [
+        pltpu.make_async_copy(src, dst, loc_sem.at[2 + i])
+        for i, (src, dst) in enumerate(
+            ((order_in, order), (freq_in, freq), (gain_in, gain), (queries, q_buf))
+        )
+    ]
     for p in range(2):
         w_local(p).start()
+    for fetch in fetches:
+        fetch.start()
+
+    @pl.when(y == 0)
+    def _():
+        pl.semaphore_wait(barrier, 10)
+
+    @pl.when(y == 1)
+    def _():
+        pl.semaphore_wait(barrier, 8)
+
+    for p in range(2):
         w_cross(p, y).start()
 
     def x_rows(b, r):
@@ -119,58 +135,68 @@
     def x_arrived(b, r):
         x_copy(0, x_rows(b, r), b, r, mate_id).wait_recv()
 
-    for r in range(PARTS):
-        x_cross(r).start()
-
-        @pl.when(even)
-        def _():
-            x_direct(r).start()
-
-    q_copy = pltpu.make_async_copy(queries, q_buf, loc_sem.at[2])
-    q_copy.start()
-
-    def w_hop(p, k, b, upward):
+    def w_hop(p, k, b, u, upward):
         chunk = at_z(-k if upward else k)
         sems = w_up if upward else w_dn
-        slot = w_slot(p, chunk, b)
-        return remote(slot, slot, sems.at[p, k, b], w_recv.at[p, chunk, b], up if upward else dn)
+        rows = 128 // SUBS
+        slot = w_buf.at[p, chunk, pl.ds(pl.multiple_of(b * 128 + u * rows, rows), rows)]
+        src = slot
+        if k == 0 and b is y:
+            src = weight.at[
+                pl.ds(u * rows, rows), pl.ds(pl.multiple_of(p * 512 + y * 256, 256), 256)
+            ]
+        return remote(
+            src, slot, sems.at[p, k, b, u], w_recv.at[p, chunk, b, u], up if upward else dn
+        )
+
+    def hops(k, u, upward):
+        if k < half - 1:
+            return True
+        return k == half - 1 and (u < SUBS // 2) == upward
 
     def ring_step(p, k):
         for b in (y, other):
-            if k == 0:
-                if b is y:
-                    w_local(p).wait()
-                else:
-                    w_cross(p, other).wait_recv()
-            else:
-                if k < half:
-                    w_hop(p, k, b, True).wait_recv()
-                w_hop(p, k, b, False).wait_recv()
-            if k < half - 1:
-                w_hop(p, k, b, True).start()
-            if k < half:
-                w_hop(p, k, b, False).start()
-
-    def slots(p, h, first, count):
-        return win.at[p, pl.ds(2 * h, 2), :, pl.ds(first * TOK, count * TOK)]
-
-    def to_up(p):
-        return remote(slots(p, y, 3, 2), slots(p, y, 1, 2), win_send.at[p, 0], win_recv.at[p, 0], up)
+            if k == 0 and b is other:
+                w_cross(p, other).wait_recv()
+            for u in range(SUBS):
+                for upward in (True, False):
+                    if k > 0 and hops(k - 1, u, upward):
+                        w_hop(p, k, b, u, upward).wait_recv()
+                    if hops(k, u, upward):
+                        w_hop(p, k, b, u, upward).start()
+
+    def slots(p, heads, first, count):
+        return win.at[p, heads, :, pl.ds(first * TOK, count * TOK)]
+
+    def pair(h):
+        return pl.ds(2 * h, 2)
+
+    def to_up(p, sub):
+        head = 2 * y + sub
+        return remote(
+            slots(p, head, 3, 2), slots(p, head, 1, 2), win_send.at[p, sub], win_recv.at[p, sub], up
+        )
 
     def to_far(p, h):
-        return remote(slots(p, y, 4, 1), slots(p, h, 0, 1), win_send.at[p, 1], win_recv.at[p, 1 + h], far)
+        return remote(
+            slots(p, pair(y), 4, 1), slots(p, pair(h), 0, 1), win_send.at[p, 2], win_recv.at[p, 2 + h], far
+        )
 
     def to_mate(p, h):
-        return remote(slots(p, h, 3, 1), slots(p, h, 3, 1), win_send.at[p, 2], win_recv.at[p, 3], mate_id)
+        both = slots(p, pair(h), 3, 1)
+        return remote(both, both, win_send.at[p, 3], win_recv.at[p, 4], mate_id)
 
     def to_mate_last(p, h):
-        return remote(slots(p, h, 4, 1), slots(p, h, 4, 1), win_send.at[p, 3], win_recv.at[p, 4], mate_id)
-
-    def to_mate_old(p, h):
-        return remote(slots(p, h, 1, 2), slots(p, h, 1, 2), win_send.at[p, 4], win_recv.at[p, 5], mate_id)
+        both = slots(p, pair(h), 4, 1)
+        return remote(both, both, win_send.at[p, 4], win_recv.at[p, 5], mate_id)
+
+    def to_mate_old(p, h, sub):
+        old = slots(p, 2 * h + sub, 1, 2)
+        return remote(old, old, win_send.at[p, 5 + sub], win_recv.at[p, 6 + sub], mate_id)
 
     def window_out(p):
-        to_up(p).start()
+        for sub in range(2):
+            to_up(p, sub).start()
         to_mate(p, y).start()
 
         @pl.when(y == 0)
@@ -179,17 +205,22 @@
 
         to_far(p, y).start()
 
-    def window_onward(p):
-        to_up(p).wait_recv()
-        to_mate_old(p, y).start()
-
-    def window_arrived(p):
+    def window_onward(p, sub):
+        to_up(p, sub).wait_recv()
+        to_mate_old(p, y, sub).start()
+
+    def own_arrived(p):
+        @pl.when(y == 0)
+        def _():
+            to_far(p, 0).wait_recv()
+
+    def others_arrived(p):
         to_mate(p, other).wait_recv()
-        to_mate_old(p, other).wait_recv()
+        for sub in range(2):
+            to_mate_old(p, other, sub).wait_recv()
 
         @pl.when(y == 0)
         def _():
-            to_far(p, 0).wait_recv()
             to_far(p, 1).wait_recv()
 
         @pl.when(y == 1)
@@ -236,18 +267,14 @@
         return jnp.dot(xn[:, columns], w_buf[p, chunk], preferred_element_type=jnp.float32)
 
     def keys():
-        acc[...] = jnp.zeros_like(acc)
-
-        def add(chunk, _):
-            acc[...] += product(0, chunk)
-            return 0
-
-        lax.fori_loop(0, ring, add, 0)
         for sub in range(2):
-            part = acc[:, sub * HD : (sub + 1) * HD]
+            part = acc[0, :, sub * HD : (sub + 1) * HD]
             turned = part * cosine[...] + pltpu.roll(part, HD // 2, 1) * sine[...]
             store(0, sub, turned)
-        acc[...] = jnp.zeros_like(acc)
+
+    def values():
+        for sub in range(2):
+            store(1, sub, acc[1, :, sub * HD : (sub + 1) * HD])
 
     def store(p, sub, rows):
         rows = rows.astype(jnp.bfloat16)
@@ -257,11 +284,16 @@
                     b * ROWS + m * TOK : b * ROWS + (m + 1) * TOK
                 ]
 
-    def value_step(k):
-        if k < half:
-            acc[...] += product(1, at_z(-k))
-        if k > 0:
-            acc[...] += product(1, at_z(k))
+    def add(p, k):
+        if k == 0:
+            w_local(p).wait()
+        total = product(p, at_z(k))
+        if 0 < k < half:
+            total += product(p, at_z(-k))
+        if k == 0:
+            acc[p] = total
+        else:
+            acc[p] += total
 
     def score(n, _):
         m = lax.rem(n, MB)
@@ -289,15 +321,6 @@
         lbuf[m] = kept
         return 0
 
-    def out_copy(n):
-        m = lax.rem(n, MB)
-        head = lax.rem(2 * y + n // MB, KVH)
-        view = (
-            pl.ds(pl.multiple_of(m * TOK, TOK), TOK),
-            pl.ds(pl.multiple_of(head * GROUP * HD, GROUP * HD), GROUP * HD),
-        )
-        return pltpu.make_async_copy(o_buf.at[view], out.at[view], out_sem.at[n])
-
     def mix(n, _):
         m = lax.rem(n, MB)
         head = lax.rem(2 * y + n // MB, KVH)
@@ -305,11 +328,10 @@
         mixed = jnp.dot(probs[n], v, preferred_element_type=jnp.float32)
         mixed = (mixed.reshape(GROUP, TOK, HD) * recip[n]).astype(jnp.bfloat16)
         for g in range(GROUP):
-            o_buf[
+            out[
                 pl.ds(pl.multiple_of(m * TOK, TOK), TOK),
                 pl.ds(pl.multiple_of((head * GROUP + g) * HD, HD), HD),
             ] = mixed[g]
-        out_copy(n).start()
         return 0
 
     def onward(r):
@@ -332,54 +354,71 @@
         if 0 <= t - LAG <= half:
             ring_step(1, t - LAG)
         if t == 0:
+            for r in range(PARTS):
+                x_cross(r).start()
+
+                @pl.when(even)
+                def _():
+                    x_direct(r).start()
+
+            for fetch in fetches[:3]:
+                fetch.wait()
             tables()
         if t == 1:
             masks()
             lbuf[...] = jnp.zeros_like(lbuf)
-        if t in (3, 5, 7, 8):
-            onward((3, 5, 7, 8).index(t))
-        if t in (9, 10):
-            for r in (2 * (t - 9), 2 * (t - 9) + 1):
+        for r in range(PARTS):
+            if t == ONWARD[r]:
+                onward(r)
+        if t == NORMED - 1:
+            for r in range(PARTS):
                 ready(other, r)
                 normalise(other, r)
-        if t in (11, 12):
-            for r in (2 * (t - 11), 2 * (t - 11) + 1):
+        if t == NORMED:
+            for r in range(PARTS):
                 ready(y, r)
                 normalise(y, r)
-        if t == 12:
-            keys()
-            window_out(0)
-            for k in range(t - LAG + 1):
-                value_step(k)
-        if t > 12:
-            value_step(t - LAG)
-        if t == 15:
-            window_onward(0)
+        for p in range(2):
+            k = t - p * LAG
+            if t == NORMED:
+                for earlier in range(k):
+                    add(p, earlier)
+            if t >= NORMED and k <= half:
+                add(p, k)
+            if k == half:
+                (keys, values)[p]()
+                window_out(p)
 
     for sub in range(2):
-        store(1, sub, acc[:, sub * HD : (sub + 1) * HD])
-    window_out(1)
-    q_copy.wait()
-    window_arrived(0)
-    lax.fori_loop(0, KVH, score, 0)
-    window_onward(1)
-    lax.fori_loop(KVH, MB * KVH, score, 0)
+        window_onward(0, sub)
+    fetches[3].wait()
+    own_arrived(0)
+    lax.fori_loop(0, 2, score, 0)
+    for sub in range(2):
+        window_onward(1, sub)
+    lax.fori_loop(2, 4, score, 0)
+    others_arrived(0)
+    lax.fori_loop(4, 8, score, 0)
     for m in range(MB):
         lse[m] = lbuf[m].T[:QH, :]
-    window_arrived(1)
-    lax.fori_loop(0, MB * KVH, mix, 0)
+    own_arrived(1)
+    lax.fori_loop(0, 4, mix, 0)
+    others_arrived(1)
+    lax.fori_loop(4, 8, mix, 0)
 
     for p in range(2):
         w_cross(p, y).wait_send()
         for k in range(half):
-            for b in range(2):
-                if k < half - 1:
-                    w_hop(p, k, b, True).wait_send()
-                w_hop(p, k, b, False).wait_send()
-        to_up(p).wait_send()
+            for b in (y, other):
+                for u in range(SUBS):
+                    for upward in (True, False):
+                        if hops(k, u, upward):
+                            w_hop(p, k, b, u, upward).wait_send()
+        for sub in range(2):
+            to_up(p, sub).wait_send()
+            to_mate_old(p, y, sub).wait_send()
         to_far(p, y).wait_send()
         to_mate(p, y).wait_send()
-        to_mate_old(p, y).wait_send()
 
         @pl.when(y == 0)
         def _():
@@ -392,9 +431,6 @@
         def _():
             x_direct(r).wait_send()
             x_onward(r).wait_send()
-
-    for n in range(MB * KVH):
-        out_copy(n).wait()
 
 
 def solution(mesh):
@@ -412,18 +448,20 @@
         out, lse = pl.pallas_call(
             functools.partial(kernel, sections, ring),
             out_shape=(
-                jax.ShapeDtypeStruct((ROWS, D), bf16),
-                jax.ShapeDtypeStruct((MB, QH, TOK), f32),
+                pltpu.VMEM((ROWS, D), bf16),
+                pltpu.VMEM((MB, QH, TOK), f32),
             ),
-            in_specs=[pl.BlockSpec(memory_space=pltpu.SMEM), vmem, vmem, any_space, any_space, any_space],
-            out_specs=(any_space, vmem),
+            in_specs=[any_space] * 6,
+            out_specs=(vmem, vmem),
             scratch_shapes=[
+                pltpu.SMEM((MB, n_ctx * 2), jnp.int32),
+                pltpu.VMEM((1, HD), f32),
+                pltpu.VMEM((1, D), bf16),
                 pltpu.VMEM((2, ROWS, D), bf16),
                 pltpu.VMEM((2 * ROWS, D), bf16),
                 pltpu.VMEM((2, ring, 256, 256), bf16),
-                pltpu.VMEM((2 * ROWS, 256), f32),
+                pltpu.VMEM((2, 2 * ROWS, 256), f32),
                 pltpu.VMEM((2, KVH, MB, WIN, HD), bf16),
-                pltpu.VMEM((ROWS, D), bf16),
                 pltpu.VMEM((ROWS, D), bf16),
                 pltpu.VMEM((MB * KVH, GROUP * TOK, SEEN), bf16),
                 pltpu.VMEM((MB * KVH, GROUP, TOK, HD), f32),
@@ -431,16 +469,15 @@
                 pltpu.VMEM((2 * ROWS, HD), f32),
                 pltpu.VMEM((MB, TOK, SEEN), f32),
                 pltpu.VMEM((MB, TOK, HD), f32),
-                dma((3,)),
-                dma((2, ring, 2)),
-                dma((2, half, 2)),
-                dma((2, half, 2)),
+                dma((6,)),
+                dma((2, ring, 2, SUBS)),
+                dma((2, half, 2, SUBS)),
+                dma((2, half, 2, SUBS)),
                 dma((2,)),
                 dma((2, PARTS)),
                 dma((3, PARTS)),
-                dma((2, 6)),
-                dma((2, 5)),
-                dma((MB * KVH,)),
+                dma((2, 8)),
+                dma((2, 7)),
             ],
             compiler_params=pltpu.CompilerParams(
                 collective_id=0, has_side_effects=True, vmem_limit_bytes=56 << 20

time: 113 us -> 87.7 us (0.78)
  the two profiles are of different devices: /device:TPU:32 before, /device:TPU:20 now
where the time goes in v2:
time: 87.7 us; the launch traced here: 87.6 us
  Pallas kernels  85.2 us (97%)
  local copies, waits for them, and re-layouts  1.76 us (2%)
    pallas_call x1, Pallas kernels, on_device(): pl.pallas_call(functools.partial(kernel, sections, ring), out_shape=(pltp...  85.2 us
    unnamed x2, local copies, waits for them, and re-layouts  1.76 us

profile of v2, /device:TPU:20, one launch (start us, length us, event | category | flops | bytes accessed | tf_op | source)
XLA Modules:
  0.0 87.6 jit_solution(6049219879949053949)
XLA Ops:
  0.6 85.2 %relay.1 = (bf16[192,4096]{1,0:T(8,128)(2,1)S(1)}, f32[2,32,96]{2,1,0:T(8,128)S(1)}) custom-call(s32[2,64]{1,0:T(2,128)} %order_in.1, f32[1,128]{1,0:T(1,128)} %constant.2.clone.freq_in, bf16[1,4096]{1,0:T(2,128)(2,1)} %gain_in.1, bf16[192,4096]{1,0:T(8,128)(2,1)} %bitcast.7, bf16[128,1024]{1,0:T(8,128)(2,1)} %bitcast.9, bf16[192,4096]{1,0:T(8,128)(2,1)} %bitcast.8), custom_call_target="tpu_custom_call" | custom-call | tf_op jit(solution)/shard_map/relay/pallas_call | solution.py:448
  85.8 1.1 %copy.10 = bf16[1,2,96,4096]{3,2,1,0:T(8,128)(2,1)} copy(bf16[1,2,96,4096]{3,2,1,0:T(8,128)(2,1)S(1)} %bitcast.5) | data formatting | bytes 3145728
  87.0 0.6 copy.11

commit v3 on v2

--- a/solution.py
+++ b/solution.py
@@ -23,8 +23,9 @@
 MESH = pl.DeviceIdType.MESH
 PARTS = 4
 PART = ROWS // PARTS
-LAG = 1
-SUBS = 2
+LAG = 0
+SUBS = 1
+XSTART = (0, 0, 1, 2)
 ONWARD = (1, 2, 3, 4)
 NORMED = 7
 LOG2E = math.log2(math.e)
@@ -55,8 +56,7 @@
 
     up = {"ctx": 2 * at_z(1) + y}
     dn = {"ctx": 2 * at_z(-1) + y}
-    far = {"ctx": 2 * at_z(2)}
-    back = at_z(-2)
+    above = {"ctx": 2 * at_z(1)}
     mate_id = {"ctx": mate}
 
     barrier = pltpu.get_barrier_semaphore()
@@ -68,14 +68,12 @@
         up, dn, mate_id,
         {"section": nxt, "ctx": c}, {"section": prv, "ctx": c},
         {"section": nxt, "ctx": mate}, {"section": prv, "ctx": mate},
-        far,
     ):
         greet(device)
 
     @pl.when(y == 0)
     def _():
-        greet({"ctx": 2 * back})
-        greet({"ctx": 2 * back + 1})
+        greet({"ctx": 2 * at_z(-1) + 1})
 
     def remote(src, dst, send, recv, device):
         return pltpu.make_async_remote_copy(
@@ -84,10 +82,10 @@
         )
 
     def w_cols(p, h):
-        return weight.at[:, pl.ds(pl.multiple_of(p * 512 + h * 256, 256), 256)]
+        return weight.at[:, :, pl.ds(pl.multiple_of(p * 512 + h * 256, 256), 256)]
 
     def w_slot(p, chunk, b):
-        return w_buf.at[p, chunk, pl.ds(pl.multiple_of(b * 128, 128), 128)]
+        return w_buf.at[p, chunk, b]
 
     def w_local(p):
         return pltpu.make_async_copy(w_cols(p, y), w_slot(p, z, y), loc_sem.at[p])
@@ -108,7 +106,7 @@
 
     @pl.when(y == 0)
     def _():
-        pl.semaphore_wait(barrier, 10)
+        pl.semaphore_wait(barrier, 7)
 
     @pl.when(y == 1)
     def _():
@@ -138,13 +136,10 @@
     def w_hop(p, k, b, u, upward):
         chunk = at_z(-k if upward else k)
         sems = w_up if upward else w_dn
-        rows = 128 // SUBS
-        slot = w_buf.at[p, chunk, pl.ds(pl.multiple_of(b * 128 + u * rows, rows), rows)]
+        slot = w_buf.at[p, chunk, b, u]
         src = slot
         if k == 0 and b is y:
-            src = weight.at[
-                pl.ds(u * rows, rows), pl.ds(pl.multiple_of(p * 512 + y * 256, 256), 256)
-            ]
+            src = w_cols(p, y).at[u]
         return remote(
             src, slot, sems.at[p, k, b, u], w_recv.at[p, chunk, b, u], up if upward else dn
         )
@@ -177,9 +172,9 @@
             slots(p, head, 3, 2), slots(p, head, 1, 2), win_send.at[p, sub], win_recv.at[p, sub], up
         )
 
-    def to_far(p, h):
+    def to_above(p, h):
         return remote(
-            slots(p, pair(y), 4, 1), slots(p, pair(h), 0, 1), win_send.at[p, 2], win_recv.at[p, 2 + h], far
+            slots(p, pair(h), 2, 1), slots(p, pair(h), 0, 1), win_send.at[p, 2], win_recv.at[p, 2 + h], above
         )
 
     def to_mate(p, h):
@@ -203,16 +198,16 @@
         def _():
             to_mate_last(p, y).start()
 
-        to_far(p, y).start()
-
     def window_onward(p, sub):
         to_up(p, sub).wait_recv()
         to_mate_old(p, y, sub).start()
+        if sub == 1:
+            to_above(p, y).start()
 
     def own_arrived(p):
         @pl.when(y == 0)
         def _():
-            to_far(p, 0).wait_recv()
+            to_above(p, 0).wait_recv()
 
     def others_arrived(p):
         to_mate(p, other).wait_recv()
@@ -221,7 +216,7 @@
 
         @pl.when(y == 0)
         def _():
-            to_far(p, 1).wait_recv()
+            to_above(p, 1).wait_recv()
 
         @pl.when(y == 1)
         def _():
@@ -264,7 +259,7 @@
 
     def product(p, chunk):
         columns = pl.ds(pl.multiple_of(chunk * 256, 256), 256)
-        return jnp.dot(xn[:, columns], w_buf[p, chunk], preferred_element_type=jnp.float32)
+        return jnp.dot(xn[:, columns], w_buf[p, chunk].reshape(256, 256), preferred_element_type=jnp.float32)
 
     def keys():
         for sub in range(2):
@@ -354,13 +349,6 @@
         if 0 <= t - LAG <= half:
             ring_step(1, t - LAG)
         if t == 0:
-            for r in range(PARTS):
-                x_cross(r).start()
-
-                @pl.when(even)
-                def _():
-                    x_direct(r).start()
-
             for fetch in fetches[:3]:
                 fetch.wait()
             tables()
@@ -368,6 +356,15 @@
             masks()
             lbuf[...] = jnp.zeros_like(lbuf)
         for r in range(PARTS):
+            if t == XSTART[r]:
+                if r > 1:
+                    x_cross(r - 2).wait_send()
+                x_cross(r).start()
+
+                @pl.when(even)
+                def _():
+                    x_direct(r).start()
+
             if t == ONWARD[r]:
                 onward(r)
         if t == NORMED - 1:
@@ -381,22 +378,20 @@
         for p in range(2):
             k = t - p * LAG
             if t == NORMED:
-                for earlier in range(k):
+                for earlier in range(min(k, half + 1)):
                     add(p, earlier)
-            if t >= NORMED and k <= half:
+            if t >= NORMED and 0 <= k <= half:
                 add(p, k)
-            if k == half:
+            if t == max(NORMED, half + p * LAG):
                 (keys, values)[p]()
                 window_out(p)
 
-    for sub in range(2):
-        window_onward(0, sub)
+    for p in range(2):
+        for sub in range(2):
+            window_onward(p, sub)
     fetches[3].wait()
     own_arrived(0)
-    lax.fori_loop(0, 2, score, 0)
-    for sub in range(2):
-        window_onward(1, sub)
-    lax.fori_loop(2, 4, score, 0)
+    lax.fori_loop(0, 4, score, 0)
     others_arrived(0)
     lax.fori_loop(4, 8, score, 0)
     for m in range(MB):
@@ -417,7 +412,7 @@
         for sub in range(2):
             to_up(p, sub).wait_send()
             to_mate_old(p, y, sub).wait_send()
-        to_far(p, y).wait_send()
+        to_above(p, y).wait_send()
         to_mate(p, y).wait_send()
 
         @pl.when(y == 0)
@@ -425,7 +420,8 @@
             to_mate_last(p, y).wait_send()
 
     for r in range(PARTS):
-        x_cross(r).wait_send()
+        if r >= PARTS - 2:
+            x_cross(r).wait_send()
 
         @pl.when(even)
         def _():
@@ -459,7 +455,7 @@
                 pltpu.VMEM((1, D), bf16),
                 pltpu.VMEM((2, ROWS, D), bf16),
                 pltpu.VMEM((2 * ROWS, D), bf16),
-                pltpu.VMEM((2, ring, 256, 256), bf16),
+                pltpu.VMEM((2, ring, 2, SUBS, 128 // SUBS, 256), bf16),
                 pltpu.VMEM((2, 2 * ROWS, 256), f32),
                 pltpu.VMEM((2, KVH, MB, WIN, HD), bf16),
                 pltpu.VMEM((ROWS, D), bf16),
@@ -484,7 +480,7 @@
             ),
             name="relay",
         )(
-            span_order, freq, norm_gain, handoff.reshape(ROWS, D), kv_weight[0], queries.reshape(ROWS, D),
+            span_order, freq, norm_gain, handoff.reshape(ROWS, D), kv_weight[0].reshape(SUBS, 128 // SUBS, 1024), queries.reshape(ROWS, D),
         )
         return out.reshape(1, MB, TOK, D), lse[None]
 

time: 87.7 us -> 84.8 us (0.967)
  the two profiles are of different devices: /device:TPU:20 before, /device:TPU:6 now
where the time goes in v3:
time: 84.8 us; the launch traced here: 84.3 us
  Pallas kernels  81.9 us (97%)
  local copies, waits for them, and re-layouts  1.76 us (2%)
    pallas_call x1, Pallas kernels, on_device(): pl.pallas_call(functools.partial(kernel, sections, ring), out_shape=(pltp...  81.9 us
    unnamed x2, local copies, waits for them, and re-layouts  1.76 us

profile of v3, /device:TPU:6, one launch (start us, length us, event | category | flops | bytes accessed | tf_op | source)
XLA Modules:
  0.0 84.3 jit_solution(28749060123343271)
XLA Ops:
  0.6 81.9 %relay.1 = (bf16[192,4096]{1,0:T(8,128)(2,1)S(1)}, f32[2,32,96]{2,1,0:T(8,128)S(1)}) custom-call(s32[2,64]{1,0:T(2,128)} %order_in.1, f32[1,128]{1,0:T(1,128)} %constant.2.clone.freq_in, bf16[1,4096]{1,0:T(2,128)(2,1)} %gain_in.1, bf16[192,4096]{1,0:T(8,128)(2,1)} %bitcast.6, bf16[1,128,1024]{2,1,0:T(8,128)(2,1)} %weight.1, bf16[192,4096]{1,0:T(8,128)(2,1)} %bitcast.7), custom_call_target="tpu_custom_call" | custom-call | tf_op jit(solution)/shard_map/relay/pallas_call | solution.py:444
  82.6 1.1 %copy.10 = bf16[1,2,96,4096]{3,2,1,0:T(8,128)(2,1)} copy(bf16[1,2,96,4096]{3,2,1,0:T(8,128)(2,1)S(1)} %bitcast.4) | data formatting | bytes 3145728
  83.7 0.6 copy.11

commit v4 on v3

--- a/solution.py
+++ b/solution.py
@@ -27,7 +27,7 @@
 SUBS = 1
 XSTART = (0, 0, 1, 2)
 ONWARD = (1, 2, 3, 4)
-NORMED = 7
+NORMED = 6
 LOG2E = math.log2(math.e)
 LN2 = math.log(2.0)
 rope_base = 500000.0
@@ -149,16 +149,17 @@
             return True
         return k == half - 1 and (u < SUBS // 2) == upward
 
-    def ring_step(p, k):
+    def ring_step(k):
         for b in (y, other):
-            if k == 0 and b is other:
-                w_cross(p, other).wait_recv()
-            for u in range(SUBS):
-                for upward in (True, False):
-                    if k > 0 and hops(k - 1, u, upward):
-                        w_hop(p, k, b, u, upward).wait_recv()
-                    if hops(k, u, upward):
-                        w_hop(p, k, b, u, upward).start()
+            for p in range(2):
+                if k == 0 and b is other:
+                    w_cross(p, other).wait_recv()
+                for u in range(SUBS):
+                    for upward in (True, False):
+                        if k > 0 and hops(k - 1, u, upward):
+                            w_hop(p, k, b, u, upward).wait_recv()
+                        if hops(k, u, upward):
+                            w_hop(p, k, b, u, upward).start()
 
     def slots(p, heads, first, count):
         return win.at[p, heads, :, pl.ds(first * TOK, count * TOK)]
@@ -344,10 +345,7 @@
             x_arrived(y, r)
 
     for t in range(LAG + half + 1):
-        if t <= half:
-            ring_step(0, t)
-        if 0 <= t - LAG <= half:
-            ring_step(1, t - LAG)
+        ring_step(t)
         if t == 0:
             for fetch in fetches[:3]:
                 fetch.wait()

time: 84.8 us -> 83.6 us (0.986)
    pallas_call x1, Pallas kernels: 81.9 us -> 81.1 us  [on_device(): pl.pallas_call(functools.partial(kernel, sections, ring), out_shape=(pltp...]
where the time goes in v4:
time: 83.6 us; the launch traced here: 83.5 us
  Pallas kernels  81.1 us (97%)
  local copies, waits for them, and re-layouts  1.76 us (2%)
    pallas_call x1, Pallas kernels, on_device(): pl.pallas_call(functools.partial(kernel, sections, ring), out_shape=(pltp...  81.1 us
    unnamed x2, local copies, waits for them, and re-layouts  1.76 us

profile of v4, /device:TPU:6, one launch (start us, length us, event | category | flops | bytes accessed | tf_op | source)
XLA Modules:
  0.0 83.5 jit_solution(9639486214677539923)
XLA Ops:
  0.6 81.1 %relay.1 = (bf16[192,4096]{1,0:T(8,128)(2,1)S(1)}, f32[2,32,96]{2,1,0:T(8,128)S(1)}) custom-call(s32[2,64]{1,0:T(2,128)} %order_in.1, f32[1,128]{1,0:T(1,128)} %constant.2.clone.freq_in, bf16[1,4096]{1,0:T(2,128)(2,1)} %gain_in.1, bf16[192,4096]{1,0:T(8,128)(2,1)} %bitcast.6, bf16[1,128,1024]{2,1,0:T(8,128)(2,1)} %weight.1, bf16[192,4096]{1,0:T(8,128)(2,1)} %bitcast.7), custom_call_target="tpu_custom_call" | custom-call | tf_op jit(solution)/shard_map/relay/pallas_call | solution.py:442
  81.7 1.1 %copy.10 = bf16[1,2,96,4096]{3,2,1,0:T(8,128)(2,1)} copy(bf16[1,2,96,4096]{3,2,1,0:T(8,128)(2,1)S(1)} %bitcast.4) | data formatting | bytes 3145728
  82.9 0.6 copy.11

commit v5 on v4

--- a/solution.py
+++ b/solution.py
@@ -191,13 +191,14 @@
         return remote(old, old, win_send.at[p, 5 + sub], win_recv.at[p, 6 + sub], mate_id)
 
     def window_out(p):
+        to_mate(p, y).start()
+
+        @pl.when(y == 0)
+        def _():
+            to_mate_last(p, y).start()
+
         for sub in range(2):
             to_up(p, sub).start()
-        to_mate(p, y).start()
-
-        @pl.when(y == 0)
-        def _():
-            to_mate_last(p, y).start()
 
     def window_onward(p, sub):
         to_up(p, sub).wait_recv()

time: 83.6 us -> 83.6 us (level)
  no operation moved by 1% of the time
where the time goes in v5:
time: 83.6 us; the launch traced here: 83.5 us
  Pallas kernels  81.1 us (97%)
  local copies, waits for them, and re-layouts  1.76 us (2%)
    pallas_call x1, Pallas kernels, on_device(): pl.pallas_call(functools.partial(kernel, sections, ring), out_shape=(pltp...  81.1 us
    unnamed x2, local copies, waits for them, and re-layouts  1.76 us

profile of v5, /device:TPU:6, one launch (start us, length us, event | category | flops | bytes accessed | tf_op | source)
XLA Modules:
  0.0 83.5 jit_solution(14755378504905244232)
XLA Ops:
  0.6 81.1 %relay.1 = (bf16[192,4096]{1,0:T(8,128)(2,1)S(1)}, f32[2,32,96]{2,1,0:T(8,128)S(1)}) custom-call(s32[2,64]{1,0:T(2,128)} %order_in.1, f32[1,128]{1,0:T(1,128)} %constant.2.clone.freq_in, bf16[1,4096]{1,0:T(2,128)(2,1)} %gain_in.1, bf16[192,4096]{1,0:T(8,128)(2,1)} %bitcast.6, bf16[1,128,1024]{2,1,0:T(8,128)(2,1)} %weight.1, bf16[192,4096]{1,0:T(8,128)(2,1)} %bitcast.7), custom_call_target="tpu_custom_call" | custom-call | tf_op jit(solution)/shard_map/relay/pallas_call | solution.py:443
  81.7 1.1 %copy.10 = bf16[1,2,96,4096]{3,2,1,0:T(8,128)(2,1)} copy(bf16[1,2,96,4096]{3,2,1,0:T(8,128)(2,1)S(1)} %bitcast.4) | data formatting | bytes 3145728
  82.9 0.6 copy.11
